TPU v7x, 256 devices: a whole 4x4x8 slice. The times are simulated.
256 devices in a mesh: dp: 4 (over x), vocab: 64 (over z, y, core).
Axes of the slice: x: 4, y: 4, z: 8, core: 2. Of those that a mesh axis runs over, the one named last changes fastest.
Arguments:
- hidden_t: bfloat16 [8192, 768], P(('dp', 'vocab')), may hold values from -6 to 6
- head: bfloat16 [8192, 81920], P('dp', 'vocab'), may hold values from -0.2 to 0.2
- teacher: bfloat16 [768, 81920], P('dp', 'vocab'), may hold values from -16 to 960
- labels: int32 [768], P('dp'), may hold values from 0 to 81919
- temps: float32 [4], replicated, may hold values from 1 to 4
- mix: float32 [2], replicated, may hold values from 0.3 to 1
Outputs:
- hidden_grad: float32 [8192, 768], P(('dp', 'vocab'))
- head_grad: bfloat16 [8192, 81920], P('dp', 'vocab')
All inputs are finite; a program needn't handle non-finite values.
Results may differ from a plain program's by a relative error of at most 0.012.
Values may be sent and summed in bfloat16 or wider, within the bound.
A program may use at most 128 MiB of HBM per device.

v0:
```python
import jax
import jax.numpy as jnp
from jax import lax
from jax.sharding import PartitionSpec as P


def shards(hidden_t, head, teacher, labels, temps, mix):
    h_block = lax.all_gather(hidden_t, "vocab", axis=0, tiled=True)
    block_width = head.shape[1]
    logits = lax.psum_scatter(
        lax.dot_general(
            h_block, head, (((0,), (0,)), ((), ())), preferred_element_type=jnp.float32
        ),
        "dp",
        scatter_dimension=0,
        tiled=True,
    )
    target = teacher.astype(jnp.float32)
    inverse = 1.0 / temps
    student = jnp.concatenate([logits[None], logits[None] * inverse[:, None, None]], axis=0)
    teacher_scaled = target[None] * inverse[:, None, None]
    stacked = jnp.concatenate([student, teacher_scaled], axis=0)
    local_peak = jnp.max(stacked, axis=2)
    highest = lax.pmax(local_peak, "vocab")
    summed = lax.psum(jnp.sum(jnp.exp(stacked - highest[:, :, None]), axis=2), "vocab")
    softmaxes = jnp.exp(stacked - highest[:, :, None]) / summed[:, :, None]
    offset = lax.axis_index("vocab") * block_width
    columns = jnp.arange(block_width, dtype=jnp.int32)[None, :] + offset
    onehot = (columns == labels[:, None]).astype(jnp.float32)
    heat_count = temps.shape[0]
    logit_grad = mix[0] * (softmaxes[0] - onehot)
    weights = mix[1] * temps
    logit_grad = logit_grad + jnp.einsum(
        "k,kab->ab", weights, softmaxes[1 : 1 + heat_count] - softmaxes[1 + heat_count :]
    )
    logit_grad = logit_grad.astype(jnp.bfloat16)
    grad_all = lax.all_gather(logit_grad, "dp", axis=0, tiled=True)
    head_grad = jnp.dot(h_block, grad_all, preferred_element_type=jnp.float32).astype(jnp.bfloat16)
    hidden_grad = lax.psum_scatter(
        lax.dot_general(
            head, grad_all, (((1,), (1,)), ((), ())), preferred_element_type=jnp.float32
        ),
        "vocab",
        scatter_dimension=0,
        tiled=True,
    )
    return (hidden_grad, head_grad)


def solution(mesh):
    placed = (P(("dp", "vocab"), None), P("dp", "vocab"), P("dp", "vocab"), P("dp"), P(), P())
    return jax.shard_map(
        shards,
        mesh=mesh,
        in_specs=placed,
        out_specs=(P(("dp", "vocab"), None), P("dp", "vocab")),
        check_vma=False,
    )
```

profile of v0, /device:TPU:6, one launch (start us, length us, event | category | flops | bytes accessed | tf_op | source)
XLA Modules:
  0.0 861.4 jit_solution(14187076467342216205)
XLA Ops:
  7.2 0.0 all-gather.3.cloned.1.call-start
  7.2 0.7 all-gather.3.cloned.1.call-update
  7.9 0.0 copy-start.3
  7.9 0.0 reduce-scatter.5.cloned.1.call-start
  8.0 83.7 %all-gather.3.cloned.1.call-done = bf16[2048,768]{1,0:T(8,128)(2,1)} async-done(((bf16[32,768]{1,0:T(8,128)(2,1)}), bf16[2048,768]{1,0:T(8,128)(2,1)}) %all-gather.3.cloned.1.call-update) | async-done | bytes 3145744 | tf_op jit(solution)/shard_map/all_gather | solution.py:8
  91.7 9.7 %fusion.14 = f32[768,1280]{1,0:T(8,128)} fusion(bf16[2048,768]{1,0:T(8,128)(2,1)} %all-gather.3.cloned.1.call-done, bf16[2048,1280]{1,0:T(8,128)(2,1)} %param.7), kind=kOutput, calls=%fused_computation.24 | convolution fusion | flops 4026531840 | bytes 12320768 | tf_op jit(solution)/shard_map/dot_general | solution.py:11
  101.3 0.0 copy-start.4
  101.3 0.0 copy-start.7
  101.3 0.0 reduce-scatter.5.cloned.1.call-update
  101.4 0.0 all-gather.5.cloned.1.call-start
  101.4 0.0 copy-done.3
  101.4 0.1 convert_element_type.15
  101.5 0.5 copy-done.4
  102.0 0.6 fusion.13
  102.6 0.0 copy-done.7
  102.7 41.7 %reduce-scatter.5.cloned.1.call-done = f32[192,1280]{1,0:T(8,128)} async-done(((f32[768,1280]{1,0:T(8,128)}), f32[192,1280]{1,0:T(8,128)}) %reduce-scatter.5.cloned.1.call-update) | async-done | bytes 983056 | tf_op jit(solution)/shard_map/reduce_scatter | solution.py:10
  144.3 0.0 copy-start.2
  144.3 2.0 broadcast_multiply_fusion.1
  146.4 0.0 copy-start
  146.4 0.0 copy-start.1
  146.4 1.8 copy-done
  148.2 1.4 copy-done.1
  149.6 0.0 copy-done.2
  149.6 0.8 fusion.5
  150.4 251.0 %pmax.7 = f32[9,192]{1,0:T(8,128)S(1)} all-reduce(f32[9,192]{1,0:T(8,128)S(1)} %fusion.5), channel_id=1, replica_groups=mesh['dp'=4,'vocab'=64] {'vocab'}, use_global_device_ids=true, to_apply=%region_2.0 | all-reduce | flops 1728 | bytes 13824 | tf_op jit(solution)/shard_map/pmax | solution.py:24
  401.4 4.3 fusion.1
  405.7 246.1 %psum.7 = f32[9,192]{1,0:T(8,128)S(1)} all-reduce(f32[9,192]{1,0:T(8,128)S(1)} %fusion.1), channel_id=1, replica_groups=mesh['dp'=4,'vocab'=64] {'vocab'}, use_global_device_ids=true, to_apply=%region_4.0 | all-reduce | flops 1728 | bytes 13824 | tf_op jit(solution)/shard_map/psum | solution.py:25
  651.8 4.6 fusion
  656.4 0.0 copy-start.5
  656.4 0.5 slice_subtract_fusion
  656.9 2.2 fusion.3
  659.1 0.0 copy-done.5
  659.2 1.7 fusion.9
  660.8 0.0 all-gather.5.cloned.1.call-update
  660.9 0.2 reduce-scatter.7.cloned.1.call-start
  661.1 26.7 %all-gather.5.cloned.1.call-done = bf16[768,1280]{1,0:T(8,128)(2,1)} async-done(((bf16[192,1280]{1,0:T(8,128)(2,1)}), bf16[768,1280]{1,0:T(8,128)(2,1)}) %all-gather.5.cloned.1.call-update) | async-done | bytes 1966096 | tf_op jit(solution)/shard_map/all_gather | solution.py:37
  687.8 10.0 %convolution_bitcast_fusion = f32[2048,768]{0,1:T(8,128)} fusion(bf16[768,1280]{1,0:T(8,128)(2,1)} %all-gather.5.cloned.1.call-done, bf16[2048,1280]{1,0:T(8,128)(2,1)} %param.7), kind=kOutput, calls=%fused_computation.9 | convolution fusion | flops 4026531840 | bytes 13500416 | tf_op jit(solution)/shard_map/dot_general | solution.py:40
  697.8 6.6 copy.16
  704.4 0.0 copy-start.6
  704.4 0.0 reduce-scatter.7.cloned.1.call-update
  704.4 1.9 copy-done.6
  706.3 7.6 fusion.2
  713.9 7.9 copy.13
  721.7 133.1 %reduce-scatter.7.cloned.1.call-done = f32[32,768]{1,0:T(8,128)} async-done(((f32[2048,768]{1,0:T(8,128)}), f32[32,768]{1,0:T(8,128)}) %reduce-scatter.7.cloned.1.call-update) | async-done | bytes 98320
  (2 shorter events, 0.0 us)
Async XLA Ops:
  7.2 84.5 %all-gather.3.cloned.1.call-start = ((), (), s32[]{:S(2)}) async-start(), calls=%async_computation.2 | async-start | bytes 3194880 | tf_op jit(solution)/shard_map/all_gather | solution.py:8
  7.9 93.5 %copy-start.3 = (bf16[192,1280]{1,0:T(8,128)(2,1)S(1)}, bf16[192,1280]{1,0:T(8,128)(2,1)}, u32[]{:S(2)}) copy-start(bf16[192,1280]{1,0:T(8,128)(2,1)} %param.8) | copy-start | bytes 1474564
  7.9 136.4 %reduce-scatter.5.cloned.1.call-start = ((), (), s32[]{:S(2)}) async-start(), calls=%async_computation.3 | async-start | bytes 4915200 | tf_op jit(solution)/shard_map/reduce_scatter | solution.py:10
  101.3 0.7 copy-start.4
  101.3 1.3 copy-start.7
  101.4 586.5 %all-gather.5.cloned.1.call-start = ((), (), s32[]{:S(2)}) async-start(), calls=%async_computation.4 | async-start | bytes 2457600 | tf_op jit(solution)/shard_map/all_gather | solution.py:37
  144.3 5.3 copy-start.2
  146.4 1.9 copy-start
  146.4 3.2 copy-start.1
  656.4 2.7 copy-start.5
  660.9 194.0 %reduce-scatter.7.cloned.1.call-start = ((), (), s32[]{:S(2)}) async-start(), calls=%async_computation.5 | async-start | bytes 6389760
  704.4 1.9 copy-start.6
Sparse Core Ops, SparseCore 0:
  10.7 80.8 all-gather.2
  101.5 42.7 reduce-scatter.4
  661.0 26.8 all-gather.4
  704.5 150.3 reduce-scatter.6
where the time goes:
time: 862 us; the launch traced here: 861 us
  blocking collectives  497 us (58%)
  waiting for transfers between devices  286 us (33%)
  matrix products  29.5 us (3%)
  local copies, waits for them, and re-layouts  20.7 us (2%)
  other arithmetic  13.9 us (2%)
  between operations  13.9 us (2%)
    pmax x1, blocking collectives, shards(): highest = lax.pmax(local_peak, 'vocab')  251 us
    psum x1, blocking collectives, shards(): lax.psum(jnp.sum(jnp.exp(stacked - highest[:, :, None]), axis=2), 'vocab')  246 us
    unnamed x5, waiting for transfers between devices  134 us
    all_gather x1, waiting for transfers between devices, shards(): h_block = lax.all_gather(hidden_t, 'vocab', axis=0, tiled=True)  83.7 us
    reduce_scatter x1, waiting for transfers between devices, shards(): lax.psum_scatter(lax.dot_general(h_block, head, (((0,), (0,)), ((), ())),...  41.7 us
    all_gather x1, waiting for transfers between devices, shards(): grad_all = lax.all_gather(logit_grad, 'dp', axis=0, tiled=True)  26.7 us
    unnamed x18, local copies, waits for them, and re-layouts  20 us
  transfers between devices with their start and end apart: 4, of which 4 were waited for; matrix products, arithmetic and copies ran while one was open for 2% of the time, Pallas kernels for 0%

commit v1 on v0

--- a/solution.py
+++ b/solution.py
@@ -22,7 +22,9 @@
     stacked = jnp.concatenate([student, teacher_scaled], axis=0)
     local_peak = jnp.max(stacked, axis=2)
     highest = lax.pmax(local_peak, "vocab")
-    summed = lax.psum(jnp.sum(jnp.exp(stacked - highest[:, :, None]), axis=2), "vocab")
+    summed = jnp.sum(
+        jax.lax.all_gather(jnp.sum(jnp.exp(stacked - highest[:, :, None]), axis=2), "vocab"), axis=0
+    )
     softmaxes = jnp.exp(stacked - highest[:, :, None]) / summed[:, :, None]
     offset = lax.axis_index("vocab") * block_width
     columns = jnp.arange(block_width, dtype=jnp.int32)[None, :] + offset

time: 862 us -> 666 us (0.77)
  blocking collectives: 497 us -> 298 us
    psum x1 -> x0, blocking collectives: 246 us -> none  [shards(): lax.psum(jnp.sum(jnp.exp(stacked - highest[:, :, None]), axis=2), 'vocab')]
    all_gather x0 -> x1, blocking collectives: none -> 47.4 us  [shards(): jax.lax.all_gather(jnp.sum(jnp.exp(stacked - highest[:, :, None]), axis=2...]
where the time goes in v1:
time: 666 us; the launch traced here: 665 us
  blocking collectives  298 us (45%)
  waiting for transfers between devices  289 us (43%)
  matrix products  29.5 us (4%)
  local copies, waits for them, and re-layouts  20.7 us (3%)
  other arithmetic  14.1 us (2%)
  between operations  13.9 us (2%)
    pmax x1, blocking collectives, shards(): highest = lax.pmax(local_peak, 'vocab')  251 us
    unnamed x5, waiting for transfers between devices  134 us
    all_gather x1, waiting for transfers between devices, shards(): h_block = lax.all_gather(hidden_t, 'vocab', axis=0, tiled=True)  83.7 us
    all_gather x1, blocking collectives, shards(): jax.lax.all_gather(jnp.sum(jnp.exp(stacked - highest[:, :, None]), axis=2...  47.4 us
    reduce_scatter x1, waiting for transfers between devices, shards(): lax.psum_scatter(lax.dot_general(h_block, head, (((0,), (0,)), ((), ())),...  41.7 us
    all_gather x1, waiting for transfers between devices, shards(): grad_all = lax.all_gather(logit_grad, 'dp', axis=0, tiled=True)  29.5 us
    unnamed x18, local copies, waits for them, and re-layouts  20 us
  transfers between devices with their start and end apart: 4, of which 4 were waited for; matrix products, arithmetic and copies ran while one was open for 2% of the time, Pallas kernels for 0%

profile of v1, /device:TPU:6, one launch (start us, length us, event | category | flops | bytes accessed | tf_op | source)
XLA Modules:
  0.0 665.2 jit_solution(7882367480892810833)
XLA Ops:
  7.2 0.0 all-gather.5.cloned.1.call-start
  7.2 0.7 all-gather.5.cloned.1.call-update
  7.9 0.0 copy-start.3
  7.9 0.0 reduce-scatter.5.cloned.1.call-start
  8.0 83.7 %all-gather.5.cloned.1.call-done = bf16[2048,768]{1,0:T(8,128)(2,1)} async-done(((bf16[32,768]{1,0:T(8,128)(2,1)}), bf16[2048,768]{1,0:T(8,128)(2,1)}) %all-gather.5.cloned.1.call-update) | async-done | bytes 3145744 | tf_op jit(solution)/shard_map/all_gather | solution.py:8
  91.7 9.7 %fusion.14 = f32[768,1280]{1,0:T(8,128)} fusion(bf16[2048,768]{1,0:T(8,128)(2,1)} %all-gather.5.cloned.1.call-done, bf16[2048,1280]{1,0:T(8,128)(2,1)} %param.7), kind=kOutput, calls=%fused_computation.24 | convolution fusion | flops 4026531840 | bytes 12320768 | tf_op jit(solution)/shard_map/dot_general | solution.py:11
  101.3 0.0 copy-start.4
  101.3 0.0 copy-start.7
  101.3 0.0 reduce-scatter.5.cloned.1.call-update
  101.4 0.0 all-gather.7.cloned.1.call-start
  101.4 0.0 copy-done.3
  101.4 0.1 convert_element_type.15
  101.5 0.5 copy-done.4
  102.0 0.6 fusion.13
  102.6 0.0 copy-done.7
  102.7 41.7 %reduce-scatter.5.cloned.1.call-done = f32[192,1280]{1,0:T(8,128)} async-done(((f32[768,1280]{1,0:T(8,128)}), f32[192,1280]{1,0:T(8,128)}) %reduce-scatter.5.cloned.1.call-update) | async-done | bytes 983056 | tf_op jit(solution)/shard_map/reduce_scatter | solution.py:10
  144.3 0.0 copy-start.2
  144.3 2.0 broadcast_multiply_fusion.1
  146.4 0.0 copy-start
  146.4 0.0 copy-start.1
  146.4 1.8 copy-done
  148.2 1.4 copy-done.1
  149.6 0.0 copy-done.2
  149.6 0.8 fusion.5
  150.4 251.0 %pmax.7 = f32[9,192]{1,0:T(8,128)S(1)} all-reduce(f32[9,192]{1,0:T(8,128)S(1)} %fusion.5), channel_id=1, replica_groups=mesh['dp'=4,'vocab'=64] {'vocab'}, use_global_device_ids=true, to_apply=%region_2.0 | all-reduce | flops 1728 | bytes 13824 | tf_op jit(solution)/shard_map/pmax | solution.py:24
  401.4 4.3 fusion.1
  405.7 47.4 %all-gather.1 = f32[64,9,192]{2,1,0:T(8,128)S(1)} all-gather(f32[1,9,192]{2,1,0:T(8,128)S(1)} %bitcast.33), channel_id=2, replica_groups=mesh['dp'=4,'vocab'=64] {'vocab'}, dimensions={0}, use_global_device_ids=true | all-gather | bytes 449280 | tf_op jit(solution)/shard_map/all_gather | solution.py:26
  453.1 0.1 reduce_sum.19
  453.2 4.6 fusion
  457.8 0.0 copy-start.5
  457.8 0.5 slice_subtract_fusion
  458.3 2.2 fusion.3
  460.5 0.0 copy-done.5
  460.5 1.7 fusion.9
  462.2 0.0 all-gather.7.cloned.1.call-update
  462.2 0.0 reduce-scatter.7.cloned.1.call-start
  462.3 29.5 %all-gather.7.cloned.1.call-done = bf16[768,1280]{1,0:T(8,128)(2,1)} async-done(((bf16[192,1280]{1,0:T(8,128)(2,1)}), bf16[768,1280]{1,0:T(8,128)(2,1)}) %all-gather.7.cloned.1.call-update) | async-done | bytes 1966096 | tf_op jit(solution)/shard_map/all_gather | solution.py:39
  491.8 10.0 %convolution_bitcast_fusion = f32[2048,768]{0,1:T(8,128)} fusion(bf16[768,1280]{1,0:T(8,128)(2,1)} %all-gather.7.cloned.1.call-done, bf16[2048,1280]{1,0:T(8,128)(2,1)} %param.7), kind=kOutput, calls=%fused_computation.9 | convolution fusion | flops 4026531840 | bytes 13500416 | tf_op jit(solution)/shard_map/dot_general | solution.py:42
  501.8 6.6 copy.16
  508.3 0.0 copy-start.6
  508.3 0.0 reduce-scatter.7.cloned.1.call-update
  508.4 1.9 copy-done.6
  510.2 7.6 %fusion.2 = bf16[2048,1280]{0,1:T(8,128)(2,1)} fusion(bf16[768,1280]{1,0:T(8,128)(2,1)} %all-gather.7.cloned.1.call-done, bf16[2048,768]{1,0:T(8,128)(2,1)S(1)} %copy-done.6), kind=kOutput, calls=%fused_computation.5 | convolution fusion | flops 4029153280 | bytes 10354688 | tf_op jit(solution)/shard_map/dot_general | solution.py:40
  517.8 7.9 %copy.13 = bf16[2048,1280]{1,0:T(8,128)(2,1)} copy(bf16[2048,1280]{0,1:T(8,128)(2,1)} %fusion.2) | data formatting | bytes 10485760
  525.7 132.9 %reduce-scatter.7.cloned.1.call-done = f32[32,768]{1,0:T(8,128)} async-done(((f32[2048,768]{1,0:T(8,128)}), f32[32,768]{1,0:T(8,128)}) %reduce-scatter.7.cloned.1.call-update) | async-done | bytes 98320
  (2 shorter events, 0.0 us)
Async XLA Ops:
  7.2 84.5 %all-gather.5.cloned.1.call-start = ((), (), s32[]{:S(2)}) async-start(), calls=%async_computation.2 | async-start | bytes 3194880 | tf_op jit(solution)/shard_map/all_gather | solution.py:8
  7.9 93.5 %copy-start.3 = (bf16[192,1280]{1,0:T(8,128)(2,1)S(1)}, bf16[192,1280]{1,0:T(8,128)(2,1)}, u32[]{:S(2)}) copy-start(bf16[192,1280]{1,0:T(8,128)(2,1)} %param.8) | copy-start | bytes 1474564
  7.9 136.4 %reduce-scatter.5.cloned.1.call-start = ((), (), s32[]{:S(2)}) async-start(), calls=%async_computation.3 | async-start | bytes 4915200 | tf_op jit(solution)/shard_map/reduce_scatter | solution.py:10
  101.3 0.7 copy-start.4
  101.3 1.3 copy-start.7
  101.4 390.4 %all-gather.7.cloned.1.call-start = ((), (), s32[]{:S(2)}) async-start(), calls=%async_computation.4 | async-start | bytes 2457600 | tf_op jit(solution)/shard_map/all_gather | solution.py:39
  144.3 5.3 copy-start.2
  146.4 1.9 copy-start
  146.4 3.2 copy-start.1
  457.8 2.7 copy-start.5
  462.2 196.4 %reduce-scatter.7.cloned.1.call-start = ((), (), s32[]{:S(2)}) async-start(), calls=%async_computation.5 | async-start | bytes 6389760
  508.3 1.9 copy-start.6
Sparse Core Ops, SparseCore 0:
  10.7 80.8 all-gather.4
  101.5 42.7 reduce-scatter.4
  462.4 29.3 all-gather.6
  508.5 150.0 reduce-scatter.6
